TPU v7x, 512 devices: a whole 4x4x16 slice. The times are simulated.
512 devices in a mesh: tile: 32 (over z_lo, y, core), date: 16 (over z_hi, x).
Axes of the slice: x: 4, y: 4, z: 16 (z_hi: 4, z_lo: 4; z = z_hi * 4 + z_lo), core: 2. Of those that a mesh axis runs over, the one named last changes fastest.
Arguments:
- secondary: bfloat16 [16, 2, 3072, 1024], P('date', None, 'tile'), may hold values from -6 to 6
- primary: bfloat16 [2, 3072, 1024], P(None, 'tile', 'date'), may hold values from -6 to 6
- margin_mask: int32 [3072], P('tile'), may hold values from 0 to 1, as said below
- az_off: int32 [16, 32], P('date', 'tile'), may hold values from -16 to 16
- rg_off: int32 [16, 32], P('date', 'tile'), may hold values from -16 to 16
- az_frac: float32 [16, 32], P('date', 'tile'), may hold values from 0 to 1
- rg_frac: float32 [16, 32], P('date', 'tile'), may hold values from 0 to 1
Outputs:
- looks: float32 [16, 2, 1536, 128], P('date', None, 'tile')
Inputs may be any that keep to these rules, and one draw needn't show every extreme that they name: `margin_mask`: ones lie only in the last 64 rows of each tile of 96 rows, and the last row of every tile is 1.
All inputs are finite; a program needn't handle non-finite values.
Results may differ from a plain program's by a relative error of at most 0.017.
Values may be sent and summed in bfloat16 or wider, within the bound.
A program may use at most 64 MiB of HBM per device.

v0:
```python
import jax
import jax.numpy as jnp
from jax import lax
from jax.sharding import PartitionSpec as P

KA = 16
LAG = 64
LA = 2
LR = 8


def padded(block, sides, width):
    for axis, dim in sides:
        count = lax.axis_size(axis)
        forward = [(i, i + 1) for i in range(count - 1)]
        backward = [(target, source) for source, target in forward]
        low = lax.ppermute(
            lax.slice_in_dim(block, block.shape[dim] - width, None, axis=dim), axis, forward
        )
        high = lax.ppermute(lax.slice_in_dim(block, 0, width, axis=dim), axis, backward)
        block = jnp.concatenate([low, block, high], axis=dim)
    return block


def passed_along(value, axis, steps):
    count = lax.axis_size(axis)
    initial, last = (max(0, -steps), min(count, count - steps))
    return lax.ppermute(value, axis, [(source, source + steps) for source in range(initial, last)])


def window(dist):
    return jnp.sinc(dist) * (0.5 + 0.5 * jnp.cos(jnp.pi * dist / 4.0))


def band_taps(offset, frac):
    inside = (offset >= -3) & (offset <= 4)
    return jnp.where(inside, window(offset.astype(jnp.float32) - frac), 0.0).astype(jnp.bfloat16)


def multilook(values):
    depth, rows_n, cols_n = values.shape
    return values.reshape(depth, rows_n // LA, LA, cols_n // LR, LR).mean(axis=(2, 4))


def shards(secondary, primary, margin_mask, az_off, rg_off, az_frac, rg_frac):
    rim_rows = KA + 4
    block_cols = 256
    image = secondary[0]
    rows_n = image.shape[1]
    cols_n = image.shape[2]
    extended = padded(image, (("tile", 1),), rim_rows)
    row_out = lax.broadcasted_iota(jnp.int32, (rows_n, rows_n + 2 * rim_rows), 0)
    row_in = lax.broadcasted_iota(jnp.int32, (rows_n, rows_n + 2 * rim_rows), 1)
    azim_taps = band_taps(row_in - row_out - az_off[0, 0] - rim_rows, az_frac[0, 0])
    azim = jnp.einsum(
        "im,kmc->kic", azim_taps, extended, preferred_element_type=jnp.float32
    ).astype(jnp.bfloat16)
    blocks_n = cols_n // block_cols
    col_pad = jnp.pad(azim, ((0, 0), (0, 0), (block_cols // 2, block_cols // 2)))
    pieces = col_pad.reshape(2, rows_n, blocks_n + 1, block_cols)
    inputs = jnp.concatenate([pieces[:, :, :-1], pieces[:, :, 1:]], axis=3)
    col_in = lax.broadcasted_iota(jnp.int32, (2 * block_cols, block_cols), 0)
    col_out = lax.broadcasted_iota(jnp.int32, (2 * block_cols, block_cols), 1)
    range_taps = band_taps(col_in - block_cols // 2 - col_out - rg_off[0, 0], rg_frac[0, 0])
    resampled = jnp.einsum("kibm,mn->kibn", inputs, range_taps, preferred_element_type=jnp.float32)
    resampled = resampled.reshape(2, rows_n, cols_n).astype(jnp.bfloat16)
    prim = lax.all_gather(primary, "date", axis=2, tiled=True)[None]
    moved = resampled[None]
    sec_f = moved.astype(jnp.float32)
    prim_f = prim.astype(jnp.float32)
    ifg_re = prim_f[:, 0] * sec_f[:, 0] + prim_f[:, 1] * sec_f[:, 1]
    ifg_im = prim_f[:, 1] * sec_f[:, 0] - prim_f[:, 0] * sec_f[:, 1]
    interf = jnp.stack((ifg_re, ifg_im), axis=1)
    upcoming = passed_along(interf[:, :, :LAG, :], "tile", -1)
    later = jnp.concatenate([interf[:, :, LAG:, :], upcoming], axis=2)
    l_re = later[:, 0]
    l_im = later[:, 1]
    weight = margin_mask.astype(jnp.float32)[None, :, None]
    e_re = jnp.sum(weight * (ifg_re * l_re + ifg_im * l_im), axis=(1, 2))
    e_im = jnp.sum(weight * (ifg_im * l_re - ifg_re * l_im), axis=(1, 2))
    power = jnp.sum(
        weight * 0.5 * (ifg_re * ifg_re + ifg_im * ifg_im + l_re * l_re + l_im * l_im), axis=(1, 2)
    )
    count = jnp.zeros_like(e_re) + jnp.sum(margin_mask.astype(jnp.float32)) * interf.shape[3]
    stats = jnp.stack((e_re, e_im, power, count), axis=1)
    totals = lax.psum(stats, "tile")
    magnitude = jnp.sqrt(totals[:, 0] * totals[:, 0] + totals[:, 1] * totals[:, 1])
    floor_val = (totals[:, 2] + 1e-06) / jnp.sqrt(jnp.maximum(totals[:, 3], 1.0))
    denom = jnp.maximum(magnitude, floor_val)
    u_re = (totals[:, 0] / denom)[:, None, None]
    u_im = (totals[:, 1] / denom)[:, None, None]
    c_re = multilook(ifg_re * u_re + ifg_im * u_im)
    c_im = multilook(ifg_im * u_re - ifg_re * u_im)
    result = jnp.stack((c_re, c_im), axis=1)
    return result


def solution(mesh):
    return jax.shard_map(
        shards,
        mesh=mesh,
        in_specs=(
            P("date", None, "tile", None),
            P(None, "tile", "date"),
            P("tile"),
            P("date", "tile"),
            P("date", "tile"),
            P("date", "tile"),
            P("date", "tile"),
        ),
        out_specs=P("date", None, "tile", None),
        check_vma=False,
    )
```

profile of v0, /device:TPU:1, one launch (start us, length us, event | category | flops | bytes accessed | tf_op | source)
XLA Modules:
  0.0 181.6 jit_solution(2312911935924852726)
XLA Ops:
  0.0 0.0 copy-start
  0.0 1.0 fusion.116
  1.0 4.6 %collective-permute-start = (bf16[2,20,1024]{2,1,0:T(8,128)(2,1)S(1)}, bf16[2,20,1024]{2,1,0:T(8,128)(2,1)S(1)}, u32[]{:S(2)}, u32[]{:S(2)}) collective-permute-start(bf16[2,20,1024]{2,1,0:T(8,128)(2,1)S(1)} %get-tuple-element.14), channel_id=1, source_target_pairs={{0,16},{16,32},{32,48},{48,64},{64,80},{80,96},{96,112},{112,128},... | collective-permute-start | bytes 245768 | tf_op jit(solution)/shard_map/ppermute | solution.py:17
  5.6 5.5 %collective-permute-start.1 = (bf16[2,20,1024]{2,1,0:T(8,128)(2,1)S(1)}, bf16[2,20,1024]{2,1,0:T(8,128)(2,1)S(1)}, u32[]{:S(2)}, u32[]{:S(2)}) collective-permute-start(bf16[2,20,1024]{2,1,0:T(8,128)(2,1)S(1)} %get-tuple-element.15), channel_id=1, source_target_pairs={{16,0},{32,16},{48,32},{64,48},{80,64},{96,80},{112,96},{128,112},... | collective-permute-start | bytes 245768 | tf_op jit(solution)/shard_map/ppermute | solution.py:20
  13.7 0.8 copy.15
  14.5 55.4 %all_gather.3 = bf16[2,96,1024]{1,0,2:T(2,128)(2,1)S(1)} all-gather(bf16[2,96,64]{1,0,2:T(2,128)(2,1)S(1)} %copy.15), channel_id=1, replica_groups=mesh['tile'=32,'date'=16] {'date'}, dimensions={2}, use_global_device_ids=true | all-gather | bytes 417792 | tf_op jit(solution)/shard_map/all_gather | solution.py:67
  69.9 0.4 copy.16
  70.3 0.1 bitcast_convert_fusion
  70.4 0.0 collective-permute-done
  70.4 0.0 collective-permute-done.1
  70.4 0.0 copy-done
  70.4 0.6 fusion.1
  71.1 0.3 copy.24
  71.3 0.1 pad.4.clone
  71.5 0.2 fusion.115
  71.7 0.2 copy.22
  71.9 0.2 copy.23
  72.1 2.9 %fusion = f32[2,96,4,256]{3,1,2,0:T(8,128)S(1)} fusion(bf16[2,96,4,256]{3,1,2,0:T(8,128)(2,1)S(1)} %copy.23, bf16[2,96,4,256]{3,1,2,0:T(8,128)(2,1)S(1)} %copy.22, f32[]{:T(128)} %bitcast.51, s32[]{:T(128)} %bitcast.49, s32[512]{0:T(512)S(1)} %iota_add_fusion), kind=kOutput, calls=%fused_computation.2 | convolution fusion | flops 209321984 | bytes 1574920 | tf_op jit(solution)/shard_map/kibm,mn->kibn/dot_general | solution.py:65
  75.0 0.5 copy.20
  75.5 0.4 reshape.581
  75.9 0.0 copy-start.1
  75.9 0.2 multiply_subtract_fusion.1
  76.1 3.9 %collective-permute-start.2 = (f32[1,2,64,1024]{3,2,1,0:T(8,128)S(1)}, f32[1,2,64,1024]{3,2,1,0:T(8,128)S(1)}, u32[]{:S(2)}, u32[]{:S(2)}) collective-permute-start(f32[1,2,64,1024]{3,2,1,0:T(8,128)S(1)} %pad_maximum_fusion.1), channel_id=1, source_target_pairs={{16,0},{32,16},{48,32},{64,48},{80,64},{96,80},{112,96},{128,112},... | collective-permute-start | bytes 1572872 | tf_op jit(solution)/shard_map/ppermute | solution.py:28
  80.0 0.0 copy-done.1
  80.0 0.6 broadcast_multiply_fusion
  81.3 12.3 %collective-permute-done.2 = f32[1,2,64,1024]{3,2,1,0:T(8,128)S(1)} collective-permute-done((f32[1,2,64,1024]{3,2,1,0:T(8,128)S(1)}, f32[1,2,64,1024]{3,2,1,0:T(8,128)S(1)}, u32[]{:S(2)}, u32[]{:S(2)}) %collective-permute-start.2) | collective-permute-done | bytes 524320 | tf_op jit(solution)/shard_map/ppermute | solution.py:28
  93.6 0.1 fusion.2
  93.7 1.0 fusion.29
  94.7 2.0 %pad_maximum_fusion.3 = f32[1,4]{1,0:T(1,128)S(1)} fusion(f32[1,1]{1,0:T(1,128)} %bitcast.18, f32[1,1]{1,0:T(1,128)} %bitcast.17, f32[1,1]{1,0:T(1,128)} %bitcast.15, f32[1,1]{1,0:T(1,128)} %bitcast.13), kind=kLoop, calls=%fused_computation.124 | loop fusion | flops 12 | bytes 32 | tf_op jit(solution)/shard_map/stack | solution.py:85
  96.6 61.0 %psum.7 = f32[1,4]{1,0:T(1,128)S(1)} all-reduce(f32[1,4]{1,0:T(1,128)S(1)} %pad_maximum_fusion.3), channel_id=1, replica_groups=mesh['tile'=32,'date'=16] {'tile'}, use_global_device_ids=true, to_apply=%region_4.5 | all-reduce | flops 4 | bytes 32 | tf_op jit(solution)/shard_map/psum | solution.py:86
  157.7 0.6 fusion.117
  163.6 0.1 multiply_add_fusion.1
  163.7 5.0 %add.275 = f32[48,2,128,8]{3,2,1,0:T(8,128)} reshape(f32[1,1,96,1024]{3,2,1,0:T(8,128)S(1)} %get-tuple-element.10) | data formatting | bytes 786432 | tf_op jit(solution)/shard_map/add | solution.py:92
  168.6 5.0 %sub.152 = f32[48,2,128,8]{3,2,1,0:T(8,128)} reshape(f32[1,1,96,1024]{3,2,1,0:T(8,128)S(1)} %get-tuple-element.11) | data formatting | bytes 786432 | tf_op jit(solution)/shard_map/sub | solution.py:93
  173.6 3.7 %reduce_sum.58 = f32[48,128]{1,0:T(8,128)S(1)} reduce(f32[48,2,128,8]{3,2,1,0:T(8,128)} %add.275, f32[]{:T(128)} %constant.55.clone.1), dimensions={1,3}, to_apply=%region_5.6 | reduce | flops 92160 | bytes 417796 | tf_op jit(solution)/shard_map/reduce_sum | solution.py:42
  177.3 3.7 %reduce_sum.59 = f32[48,128]{1,0:T(8,128)S(1)} reduce(f32[48,2,128,8]{3,2,1,0:T(8,128)} %sub.152, f32[]{:T(128)} %constant.55.clone.1), dimensions={1,3}, to_apply=%region_6.7 | reduce | flops 92160 | bytes 417796 | tf_op jit(solution)/shard_map/reduce_sum | solution.py:42
  181.0 0.6 pad_maximum_fusion.2
  (4 shorter events, 0.1 us)
Async XLA Ops:
  0.0 70.4 %copy-start = (bf16[1,2,96,1024]{3,2,1,0:T(8,128)(2,1)S(1)}, bf16[1,2,96,1024]{3,2,1,0:T(8,128)(2,1)}, u32[]{:S(2)}) copy-start(bf16[1,2,96,1024]{3,2,1,0:T(8,128)(2,1)} %param.7) | copy-start | bytes 1179652
  1.0 69.4 %collective-permute-start = (bf16[2,20,1024]{2,1,0:T(8,128)(2,1)S(1)}, bf16[2,20,1024]{2,1,0:T(8,128)(2,1)S(1)}, u32[]{:S(2)}, u32[]{:S(2)}) collective-permute-start(bf16[2,20,1024]{2,1,0:T(8,128)(2,1)S(1)} %get-tuple-element.14), channel_id=1, source_target_pairs={{0,16},{16,32},{32,48},{48,64},{64,80},{80,96},{96,112},{112,128},... | collective-permute-start | bytes 245768 | tf_op jit(solution)/shard_map/ppermute | solution.py:17
  5.6 64.8 %collective-permute-start.1 = (bf16[2,20,1024]{2,1,0:T(8,128)(2,1)S(1)}, bf16[2,20,1024]{2,1,0:T(8,128)(2,1)S(1)}, u32[]{:S(2)}, u32[]{:S(2)}) collective-permute-start(bf16[2,20,1024]{2,1,0:T(8,128)(2,1)S(1)} %get-tuple-element.15), channel_id=1, source_target_pairs={{16,0},{32,16},{48,32},{64,48},{80,64},{96,80},{112,96},{128,112},... | collective-permute-start | bytes 245768 | tf_op jit(solution)/shard_map/ppermute | solution.py:20
  75.9 4.1 %copy-start.1 = (s32[96]{0:T(128)S(1)}, s32[96]{0:T(128)}, u32[]{:S(2)}) copy-start(s32[96]{0:T(128)} %param.9) | copy-start | bytes 1156
  76.1 17.5 %collective-permute-start.2 = (f32[1,2,64,1024]{3,2,1,0:T(8,128)S(1)}, f32[1,2,64,1024]{3,2,1,0:T(8,128)S(1)}, u32[]{:S(2)}, u32[]{:S(2)}) collective-permute-start(f32[1,2,64,1024]{3,2,1,0:T(8,128)S(1)} %pad_maximum_fusion.1), channel_id=1, source_target_pairs={{16,0},{32,16},{48,32},{64,48},{80,64},{96,80},{112,96},{128,112},... | collective-permute-start | bytes 1572872 | tf_op jit(solution)/shard_map/ppermute | solution.py:28
where the time goes:
time: 182 us
  blocking collectives  116 us (64%)
  local copies, waits for them, and re-layouts  14.7 us (8%)
  starting transfers between devices  13.9 us (8%)
  waiting for transfers between devices  12.3 us (7%)
  other arithmetic  12 us (7%)
  between operations  8.73 us (5%)
  matrix products  3.52 us (2%)
    psum x1, blocking collectives, shards(): totals = lax.psum(stats, 'tile')  61 us
    all_gather x1, blocking collectives, shards(): prim = lax.all_gather(primary, 'date', axis=2, tiled=True)[None]  55.4 us
    ppermute x1, waiting for transfers between devices, passed_along(): lax.ppermute(value, axis, [(source, source + steps) for source in range(i...  12.3 us
    reduce_sum x2, other arithmetic, multilook(): values.reshape(depth, rows_n // LA, LA, cols_n // LR, LR).mean(axis=(2, 4))  7.34 us
    ppermute x1, starting transfers between devices, padded(): lax.ppermute(lax.slice_in_dim(block, 0, width, axis=dim), axis, backward)  5.46 us
    sub x1, local copies, waits for them, and re-layouts, shards(): c_im = multilook(ifg_im * u_re - ifg_re * u_im)  4.97 us
    add x1, local copies, waits for them, and re-layouts, shards(): c_re = multilook(ifg_re * u_re + ifg_im * u_im)  4.95 us
    ppermute x1, starting transfers between devices, padded(): lax.ppermute(lax.slice_in_dim(block, block.shape[dim] - width, None, axis...  4.58 us
  transfers between devices with their start and end apart: 3, of which 1 were waited for; matrix products, arithmetic and copies ran while one was open for 1% of the time, Pallas kernels for 0%

commit v1 on v0

--- a/solution.py
+++ b/solution.py
@@ -83,7 +83,7 @@
     )
     count = jnp.zeros_like(e_re) + jnp.sum(margin_mask.astype(jnp.float32)) * interf.shape[3]
     stats = jnp.stack((e_re, e_im, power, count), axis=1)
-    totals = lax.psum(stats, "tile")
+    totals = jnp.sum(lax.all_gather(stats, "tile"), axis=0)
     magnitude = jnp.sqrt(totals[:, 0] * totals[:, 0] + totals[:, 1] * totals[:, 1])
     floor_val = (totals[:, 2] + 1e-06) / jnp.sqrt(jnp.maximum(totals[:, 3], 1.0))
     denom = jnp.maximum(magnitude, floor_val)

time: 182 us -> 159 us (0.87)
  blocking collectives: 116 us -> 93.3 us
    psum x1 -> x0, blocking collectives: 61 us -> none  [shards(): totals = lax.psum(stats, 'tile')]
    all_gather x0 -> x1, blocking collectives: none -> 37.9 us  [shards(): totals = jnp.sum(lax.all_gather(stats, 'tile'), axis=0)]
    another operation x1 -> x0, other arithmetic: 1.95 us -> none  [shards(): stats = jnp.stack((e_re, e_im, power, count), axis=1)]
    unnamed x0 -> x1, other arithmetic: none -> 1.95 us
where the time goes in v1:
time: 159 us
  blocking collectives  93.3 us (59%)
  local copies, waits for them, and re-layouts  14.7 us (9%)
  starting transfers between devices  13.9 us (9%)
  waiting for transfers between devices  12.3 us (8%)
  other arithmetic  12 us (8%)
  between operations  8.73 us (5%)
  matrix products  3.52 us (2%)
    all_gather x1, blocking collectives, shards(): prim = lax.all_gather(primary, 'date', axis=2, tiled=True)[None]  55.4 us
    all_gather x1, blocking collectives, shards(): totals = jnp.sum(lax.all_gather(stats, 'tile'), axis=0)  37.9 us
    ppermute x1, waiting for transfers between devices, passed_along(): lax.ppermute(value, axis, [(source, source + steps) for source in range(i...  12.3 us
    reduce_sum x2, other arithmetic, multilook(): values.reshape(depth, rows_n // LA, LA, cols_n // LR, LR).mean(axis=(2, 4))  7.33 us
    ppermute x1, starting transfers between devices, padded(): lax.ppermute(lax.slice_in_dim(block, 0, width, axis=dim), axis, backward)  5.46 us
    add x1, local copies, waits for them, and re-layouts, shards(): c_re = multilook(ifg_re * u_re + ifg_im * u_im)  5 us
    sub x1, local copies, waits for them, and re-layouts, shards(): c_im = multilook(ifg_im * u_re - ifg_re * u_im)  5 us
    ppermute x1, starting transfers between devices, padded(): lax.ppermute(lax.slice_in_dim(block, block.shape[dim] - width, None, axis...  4.58 us
  transfers between devices with their start and end apart: 3, of which 1 were waited for; matrix products, arithmetic and copies ran while one was open for 1% of the time, Pallas kernels for 0%

profile of v1, /device:TPU:1, one launch (start us, length us, event | category | flops | bytes accessed | tf_op | source)
XLA Modules:
  0.0 158.6 jit_solution(8683836538032469670)
XLA Ops:
  0.0 0.0 copy-start
  0.0 1.0 fusion.116
  1.0 4.6 %collective-permute-start = (bf16[2,20,1024]{2,1,0:T(8,128)(2,1)S(1)}, bf16[2,20,1024]{2,1,0:T(8,128)(2,1)S(1)}, u32[]{:S(2)}, u32[]{:S(2)}) collective-permute-start(bf16[2,20,1024]{2,1,0:T(8,128)(2,1)S(1)} %get-tuple-element.14), channel_id=1, source_target_pairs={{0,16},{16,32},{32,48},{48,64},{64,80},{80,96},{96,112},{112,128},... | collective-permute-start | bytes 245768 | tf_op jit(solution)/shard_map/ppermute | solution.py:17
  5.6 5.5 %collective-permute-start.1 = (bf16[2,20,1024]{2,1,0:T(8,128)(2,1)S(1)}, bf16[2,20,1024]{2,1,0:T(8,128)(2,1)S(1)}, u32[]{:S(2)}, u32[]{:S(2)}) collective-permute-start(bf16[2,20,1024]{2,1,0:T(8,128)(2,1)S(1)} %get-tuple-element.15), channel_id=1, source_target_pairs={{16,0},{32,16},{48,32},{64,48},{80,64},{96,80},{112,96},{128,112},... | collective-permute-start | bytes 245768 | tf_op jit(solution)/shard_map/ppermute | solution.py:20
  13.7 0.8 copy.15
  14.5 55.4 %all_gather.9 = bf16[2,96,1024]{1,0,2:T(2,128)(2,1)S(1)} all-gather(bf16[2,96,64]{1,0,2:T(2,128)(2,1)S(1)} %copy.15), channel_id=1, replica_groups=mesh['tile'=32,'date'=16] {'date'}, dimensions={2}, use_global_device_ids=true | all-gather | bytes 417792 | tf_op jit(solution)/shard_map/all_gather | solution.py:67
  69.9 0.4 copy.16
  70.3 0.1 bitcast_convert_fusion
  70.4 0.0 collective-permute-done
  70.4 0.0 collective-permute-done.1
  70.4 0.0 copy-done
  70.4 0.6 fusion.1
  71.1 0.3 copy.24
  71.3 0.1 pad.4.clone
  71.5 0.2 fusion.115
  71.7 0.2 copy.22
  71.9 0.2 copy.23
  72.1 2.9 %fusion = f32[2,96,4,256]{3,1,2,0:T(8,128)S(1)} fusion(bf16[2,96,4,256]{3,1,2,0:T(8,128)(2,1)S(1)} %copy.23, bf16[2,96,4,256]{3,1,2,0:T(8,128)(2,1)S(1)} %copy.22, f32[]{:T(128)} %bitcast.54, s32[]{:T(128)} %bitcast.52, s32[512]{0:T(512)S(1)} %iota_add_fusion), kind=kOutput, calls=%fused_computation.2 | convolution fusion | flops 209321984 | bytes 1574920 | tf_op jit(solution)/shard_map/kibm,mn->kibn/dot_general | solution.py:65
  75.0 0.5 copy.20
  75.5 0.4 reshape.582
  75.9 0.0 copy-start.1
  75.9 0.2 multiply_subtract_fusion.1
  76.1 3.9 %collective-permute-start.2 = (f32[1,2,64,1024]{3,2,1,0:T(8,128)S(1)}, f32[1,2,64,1024]{3,2,1,0:T(8,128)S(1)}, u32[]{:S(2)}, u32[]{:S(2)}) collective-permute-start(f32[1,2,64,1024]{3,2,1,0:T(8,128)S(1)} %pad_maximum_fusion.1), channel_id=1, source_target_pairs={{16,0},{32,16},{48,32},{64,48},{80,64},{96,80},{112,96},{128,112},... | collective-permute-start | bytes 1572872 | tf_op jit(solution)/shard_map/ppermute | solution.py:28
  80.0 0.0 copy-done.1
  80.0 0.6 broadcast_multiply_fusion
  81.3 12.3 %collective-permute-done.2 = f32[1,2,64,1024]{3,2,1,0:T(8,128)S(1)} collective-permute-done((f32[1,2,64,1024]{3,2,1,0:T(8,128)S(1)}, f32[1,2,64,1024]{3,2,1,0:T(8,128)S(1)}, u32[]{:S(2)}, u32[]{:S(2)}) %collective-permute-start.2) | collective-permute-done | bytes 524320 | tf_op jit(solution)/shard_map/ppermute | solution.py:28
  93.6 0.1 fusion.2
  93.7 1.0 fusion.29
  94.7 2.0 %maximum_bitcast_fusion = f32[1,1,4]{2,1,0:T(1,128)S(1)} fusion(f32[1,1]{1,0:T(1,128)} %bitcast.18, f32[1,1]{1,0:T(1,128)} %bitcast.17, f32[1,1]{1,0:T(1,128)} %bitcast.15, f32[1,1]{1,0:T(1,128)} %bitcast.13), kind=kLoop, calls=%fused_computation.124 | loop fusion | flops 12 | bytes 32
  96.6 37.9 %all-gather.1 = f32[32,1,4]{2,1,0:T(1,128)S(1)} all-gather(f32[1,1,4]{2,1,0:T(1,128)S(1)} %maximum_bitcast_fusion), channel_id=2, replica_groups=mesh['tile'=32,'date'=16] {'tile'}, dimensions={0}, use_global_device_ids=true | all-gather | bytes 528 | tf_op jit(solution)/shard_map/all_gather | solution.py:86
  134.5 0.1 reduce.8
  134.6 0.6 fusion.117
  140.5 0.1 multiply_add_fusion.1
  140.6 5.0 %add.273 = f32[48,2,128,8]{3,2,1,0:T(8,128)} reshape(f32[1,1,96,1024]{3,2,1,0:T(8,128)S(1)} %get-tuple-element.10) | data formatting | bytes 786432 | tf_op jit(solution)/shard_map/add | solution.py:92
  145.6 3.7 %reduce_sum.71 = f32[48,128]{1,0:T(8,128)S(1)} reduce(f32[48,2,128,8]{3,2,1,0:T(8,128)} %add.273, f32[]{:T(128)} %constant.55.clone.1), dimensions={1,3}, to_apply=%region_5.6 | reduce | flops 92160 | bytes 417796 | tf_op jit(solution)/shard_map/reduce_sum | solution.py:42
  149.3 5.0 %sub.152 = f32[48,2,128,8]{3,2,1,0:T(8,128)} reshape(f32[1,1,96,1024]{3,2,1,0:T(8,128)S(1)} %get-tuple-element.11) | data formatting | bytes 786432 | tf_op jit(solution)/shard_map/sub | solution.py:93
  154.3 3.7 %reduce_sum.72 = f32[48,128]{1,0:T(8,128)S(1)} reduce(f32[48,2,128,8]{3,2,1,0:T(8,128)} %sub.152, f32[]{:T(128)} %constant.55.clone.1), dimensions={1,3}, to_apply=%region_6.7 | reduce | flops 92160 | bytes 417796 | tf_op jit(solution)/shard_map/reduce_sum | solution.py:42
  157.9 0.6 pad_maximum_fusion.2
  (4 shorter events, 0.1 us)
Async XLA Ops:
  0.0 70.4 %copy-start = (bf16[1,2,96,1024]{3,2,1,0:T(8,128)(2,1)S(1)}, bf16[1,2,96,1024]{3,2,1,0:T(8,128)(2,1)}, u32[]{:S(2)}) copy-start(bf16[1,2,96,1024]{3,2,1,0:T(8,128)(2,1)} %param.7) | copy-start | bytes 1179652
  1.0 69.4 %collective-permute-start = (bf16[2,20,1024]{2,1,0:T(8,128)(2,1)S(1)}, bf16[2,20,1024]{2,1,0:T(8,128)(2,1)S(1)}, u32[]{:S(2)}, u32[]{:S(2)}) collective-permute-start(bf16[2,20,1024]{2,1,0:T(8,128)(2,1)S(1)} %get-tuple-element.14), channel_id=1, source_target_pairs={{0,16},{16,32},{32,48},{48,64},{64,80},{80,96},{96,112},{112,128},... | collective-permute-start | bytes 245768 | tf_op jit(solution)/shard_map/ppermute | solution.py:17
  5.6 64.8 %collective-permute-start.1 = (bf16[2,20,1024]{2,1,0:T(8,128)(2,1)S(1)}, bf16[2,20,1024]{2,1,0:T(8,128)(2,1)S(1)}, u32[]{:S(2)}, u32[]{:S(2)}) collective-permute-start(bf16[2,20,1024]{2,1,0:T(8,128)(2,1)S(1)} %get-tuple-element.15), channel_id=1, source_target_pairs={{16,0},{32,16},{48,32},{64,48},{80,64},{96,80},{112,96},{128,112},... | collective-permute-start | bytes 245768 | tf_op jit(solution)/shard_map/ppermute | solution.py:20
  75.9 4.1 %copy-start.1 = (s32[96]{0:T(128)S(1)}, s32[96]{0:T(128)}, u32[]{:S(2)}) copy-start(s32[96]{0:T(128)} %param.9) | copy-start | bytes 1156
  76.1 17.5 %collective-permute-start.2 = (f32[1,2,64,1024]{3,2,1,0:T(8,128)S(1)}, f32[1,2,64,1024]{3,2,1,0:T(8,128)S(1)}, u32[]{:S(2)}, u32[]{:S(2)}) collective-permute-start(f32[1,2,64,1024]{3,2,1,0:T(8,128)S(1)} %pad_maximum_fusion.1), channel_id=1, source_target_pairs={{16,0},{32,16},{48,32},{64,48},{80,64},{96,80},{112,96},{128,112},... | collective-permute-start | bytes 1572872 | tf_op jit(solution)/shard_map/ppermute | solution.py:28
